TPU v7x, 32 devices: a whole 2x2x4 slice. The times are simulated.
32 devices in a mesh: rep: 4 (over y, x), shard: 8 (over z, core).
Axes of the slice: x: 2, y: 2, z: 4, core: 2. Of those that a mesh axis runs over, the one named last changes fastest.
Arguments:
- hidden_in: float32 [4096, 768], P(('rep', 'shard')), may hold values from -6 to 6
- doc_ids: int32 [32, 128], P(('rep', 'shard')), may hold values from 0 to 3, never falling along the last dimension, each value on 1 to 64 neighbouring positions
- cotangent: float32 [4096, 768], P(('rep', 'shard')), may hold values from -6 to 6
- pre_gain: float32 [1, 768], P(None, 'shard'), may hold values from 0.25 to 1.75
- pre_shift: float32 [1, 768], P(None, 'shard'), may hold values from -3 to 3
- qkv_weight: float32 [1, 768, 2304], P(None, 'shard'), may hold values from -0.21875 to 0.21875
- query_bias: float32 [1, 768], P(None, 'shard'), may hold values from -3 to 3
- value_bias: float32 [1, 768], P(None, 'shard'), may hold values from -3 to 3
- out_weight: float32 [1, 768, 768], P(None, 'shard'), may hold values from -0.875 to 0.875
- out_bias: float32 [1, 768], P(None, 'shard'), may hold values from -3 to 3
- post_gain: float32 [1, 768], P(None, 'shard'), may hold values from 0.25 to 1.75
- post_shift: float32 [1, 768], P(None, 'shard'), may hold values from -3 to 3
- up_weight: float32 [1, 768, 3072], P(None, 'shard'), may hold values from -0.21875 to 0.21875
- up_bias: float32 [1, 3072], P(None, 'shard'), may hold values from -3 to 3
- down_weight: float32 [1, 3072, 768], P(None, 'shard'), may hold values from -0.109375 to 0.109375
- down_bias: float32 [1, 768], P(None, 'shard'), may hold values from -3 to 3
Outputs:
- hidden_out: float32 [4096, 768], P(('rep', 'shard'))
- input_grad: float32 [4096, 768], P(('rep', 'shard'))
- grad_pre_gain: float32 [1, 768], P(None, 'shard')
- grad_pre_shift: float32 [1, 768], P(None, 'shard')
- grad_qkv_weight: float32 [1, 768, 2304], P(None, 'shard')
- grad_query_bias: float32 [1, 768], P(None, 'shard')
- grad_value_bias: float32 [1, 768], P(None, 'shard')
- grad_out_weight: float32 [1, 768, 768], P(None, 'shard')
- grad_out_bias: float32 [1, 768], P(None, 'shard')
- grad_post_gain: float32 [1, 768], P(None, 'shard')
- grad_post_shift: float32 [1, 768], P(None, 'shard')
- grad_up_weight: float32 [1, 768, 3072], P(None, 'shard')
- grad_up_bias: float32 [1, 3072], P(None, 'shard')
- grad_down_weight: float32 [1, 3072, 768], P(None, 'shard')
- grad_down_bias: float32 [1, 768], P(None, 'shard')
Inputs may be any that keep to these rules, and one draw needn't show every extreme that they name: `doc_ids`: along each row the document number never falls; all 4 documents appear in every row, each of 1 to 64 tokens, one of exactly 64.
All inputs are finite; a program needn't handle non-finite values.
Results may differ from a plain program's by a relative error of at most 0.018.
Values may be sent and summed in bfloat16 or wider, within the bound.
No kernel may reach another device: no remote copies, remote signals or barrier semaphores. Data moves between devices by JAX's collectives and lax.ppermute only.
A program may use at most 128 MiB of HBM per device.

v0:
```python
import jax
import jax.numpy as jnp
from jax import lax
from jax.sharding import PartitionSpec as P

HEADS = 12
HEAD = 64
LAYERS = 1
EPS = 1e-05
GELU_C = 0.7978845608028654
NEG_FILL = -1e30


def norm(values_in, gains, shifts):
    average = jnp.mean(values_in, axis=-1, keepdims=True)
    centred = values_in - average
    spread = jnp.mean(centred * centred, axis=-1, keepdims=True)
    return centred * lax.rsqrt(spread + EPS) * gains + shifts


def gelu_tanh(values_in):
    return (
        0.5
        * values_in
        * (1.0 + jnp.tanh(GELU_C * (values_in + 0.044715 * values_in * values_in * values_in)))
    )


def project(left, right):
    return jnp.dot(left, right, preferred_element_type=jnp.float32)


def project_back(left, right):
    return lax.dot_general(
        left, right, (((0,), (0,)), ((), ())), preferred_element_type=jnp.float32
    )


def project_trans(left, right):
    return lax.dot_general(
        left, right, (((1,), (1,)), ((), ())), preferred_element_type=jnp.float32
    )


def layer_slices(shards, layer_index):
    return tuple((stacked[layer_index].astype(jnp.bfloat16) for stacked in shards))


def fetch_forward(shards, layer_index):
    parts = layer_slices(shards, layer_index)
    return (
        lax.all_gather(parts[0], "shard", axis=0, tiled=True),
        lax.all_gather(parts[1], "shard", axis=0, tiled=True),
        lax.all_gather(parts[2], "shard", axis=0, tiled=True),
        lax.all_gather(parts[3], "shard", axis=0, tiled=True),
        lax.all_gather(parts[4], "shard", axis=0, tiled=True),
        lax.all_gather(parts[5], "shard", axis=0, tiled=True),
        lax.all_gather(parts[6], "shard", axis=0, tiled=True),
        lax.all_gather(parts[7], "shard", axis=0, tiled=True),
        lax.all_gather(parts[8], "shard", axis=0, tiled=True),
        lax.all_gather(parts[9], "shard", axis=0, tiled=True),
        lax.all_gather(parts[10], "shard", axis=0, tiled=True),
        lax.all_gather(parts[11], "shard", axis=0, tiled=True),
        lax.all_gather(parts[12], "shard", axis=0, tiled=True),
    )


def reduce_nested_rest(grads):
    owned = (
        lax.psum_scatter(
            grads[0].astype(jnp.bfloat16), "shard", scatter_dimension=0, tiled=True
        ).astype(jnp.float32),
        lax.psum_scatter(
            grads[1].astype(jnp.bfloat16), "shard", scatter_dimension=0, tiled=True
        ).astype(jnp.float32),
        lax.psum_scatter(
            grads[2].astype(jnp.bfloat16), "shard", scatter_dimension=0, tiled=True
        ).astype(jnp.float32),
        lax.psum_scatter(
            grads[3].astype(jnp.bfloat16), "shard", scatter_dimension=0, tiled=True
        ).astype(jnp.float32),
        lax.psum_scatter(
            grads[4].astype(jnp.bfloat16), "shard", scatter_dimension=0, tiled=True
        ).astype(jnp.float32),
        lax.psum_scatter(
            grads[5].astype(jnp.bfloat16), "shard", scatter_dimension=0, tiled=True
        ).astype(jnp.float32),
        lax.psum_scatter(
            grads[6].astype(jnp.bfloat16), "shard", scatter_dimension=0, tiled=True
        ).astype(jnp.float32),
        lax.psum_scatter(
            grads[7].astype(jnp.bfloat16), "shard", scatter_dimension=0, tiled=True
        ).astype(jnp.float32),
        lax.psum_scatter(
            grads[8].astype(jnp.bfloat16), "shard", scatter_dimension=0, tiled=True
        ).astype(jnp.float32),
        lax.psum_scatter(
            grads[9].astype(jnp.bfloat16), "shard", scatter_dimension=0, tiled=True
        ).astype(jnp.float32),
        lax.psum_scatter(
            grads[10].astype(jnp.bfloat16), "shard", scatter_dimension=0, tiled=True
        ).astype(jnp.float32),
    )
    return (
        lax.psum(owned[0].astype(jnp.bfloat16), "rep").astype(jnp.float32),
        lax.psum(owned[1].astype(jnp.bfloat16), "rep").astype(jnp.float32),
        lax.psum(owned[2].astype(jnp.bfloat16), "rep").astype(jnp.float32),
        lax.psum(owned[3].astype(jnp.bfloat16), "rep").astype(jnp.float32),
        lax.psum(owned[4].astype(jnp.bfloat16), "rep").astype(jnp.float32),
        lax.psum(owned[5].astype(jnp.bfloat16), "rep").astype(jnp.float32),
        lax.psum(owned[6].astype(jnp.bfloat16), "rep").astype(jnp.float32),
        lax.psum(owned[7].astype(jnp.bfloat16), "rep").astype(jnp.float32),
        lax.psum(owned[8].astype(jnp.bfloat16), "rep").astype(jnp.float32),
        lax.psum(owned[9].astype(jnp.bfloat16), "rep").astype(jnp.float32),
        lax.psum(owned[10].astype(jnp.bfloat16), "rep").astype(jnp.float32),
    )


def block_scores(query_block, key_rows, doc_block, doc_row, offset):
    query_places = offset + lax.iota(jnp.int32, query_block.shape[0])
    key_places = lax.iota(jnp.int32, key_rows.shape[0])
    allowed = (query_places[:, None] >= key_places[None, :]) & (
        doc_block[:, None] == doc_row[None, :]
    )
    scores = (
        jnp.einsum("qhe,khe->hqk", query_block, key_rows, preferred_element_type=jnp.float32)
        * 0.125
    )
    return jnp.where(allowed[None], scores, NEG_FILL)


def attention_forward(queries, key_rows, value_rows, doc_row):
    length = queries.shape[0]
    rows_block = min(length, 512)
    blocks = length // rows_block

    def one_block(block_index):
        offset = block_index * rows_block
        scores = block_scores(queries, key_rows, doc_row, doc_row, offset)
        highest = jnp.max(scores, axis=-1, keepdims=True)
        log_total = highest + jnp.log(jnp.sum(jnp.exp(scores - highest), axis=-1, keepdims=True))
        weights = jnp.exp(scores - log_total).astype(jnp.bfloat16)
        mixed = jnp.einsum("hqk,khe->qhe", weights, value_rows, preferred_element_type=jnp.float32)
        return (mixed.astype(jnp.bfloat16), log_total)

    mixed, log_totals = lax.map(one_block, jnp.arange(blocks, dtype=jnp.int32))
    return (mixed.reshape(length, -1), log_totals)


def attention_backward(queries, key_rows, value_rows, doc_row, log_totals, grad_mixed):
    length = queries.shape[0]
    rows_block = min(length, 512)
    blocks = length // rows_block

    def one_block(carry, block_index):
        grad_keys, grad_values = carry
        offset = block_index * rows_block
        scores = block_scores(queries, key_rows, doc_row, doc_row, offset)
        weights = jnp.exp(scores - log_totals[block_index])
        grad_values = grad_values + jnp.einsum(
            "hqk,qhe->khe",
            weights.astype(jnp.bfloat16),
            grad_mixed,
            preferred_element_type=jnp.float32,
        )
        grad_weights = jnp.einsum(
            "qhe,khe->hqk", grad_mixed, value_rows, preferred_element_type=jnp.float32
        )
        grad_scores = weights * (
            grad_weights - jnp.sum(grad_weights * weights, axis=-1, keepdims=True)
        )
        grad_scores = grad_scores.astype(jnp.bfloat16)
        grad_query = (
            jnp.einsum("hqk,khe->qhe", grad_scores, key_rows, preferred_element_type=jnp.float32)
            * 0.125
        )
        grad_keys = (
            grad_keys
            + jnp.einsum("hqk,qhe->khe", grad_scores, queries, preferred_element_type=jnp.float32)
            * 0.125
        )
        return ((grad_keys, grad_values), grad_query)

    zeros_kv = jnp.zeros(key_rows.shape, jnp.float32)
    (grad_keys, grad_values), grad_queries = lax.scan(
        one_block, (zeros_kv, zeros_kv), jnp.arange(blocks, dtype=jnp.int32)
    )
    return (
        grad_queries.reshape(length, -1),
        grad_keys.reshape(length, -1),
        grad_values.reshape(length, -1),
    )


def layer_forward(hidden, weights, doc_row):
    (
        pre_gain,
        pre_shift,
        qkv_weight,
        query_bias,
        value_bias,
        out_weight,
        out_bias,
        post_gain,
        post_shift,
        up_weight,
        up_bias,
        down_weight,
        down_bias,
    ) = weights
    rows_here = hidden.shape[0]
    normed = norm(hidden, pre_gain.astype(jnp.float32), pre_shift.astype(jnp.float32)).astype(
        jnp.bfloat16
    )
    bias_row = jnp.concatenate([query_bias, jnp.zeros_like(query_bias), value_bias]).astype(
        jnp.float32
    )
    packed = (project(normed, qkv_weight) + bias_row).astype(jnp.bfloat16)
    shaped = packed.reshape(rows_here, 3, HEADS, HEAD)
    mixed, log_totals = attention_forward(shaped[:, 0], shaped[:, 1], shaped[:, 2], doc_row)
    middle = hidden + project(mixed, out_weight) + out_bias.astype(jnp.float32)
    normed_two = norm(middle, post_gain.astype(jnp.float32), post_shift.astype(jnp.float32)).astype(
        jnp.bfloat16
    )
    pre_act = project(normed_two, up_weight) + up_bias.astype(jnp.float32)
    activ = gelu_tanh(pre_act).astype(jnp.bfloat16)
    output = middle + project(activ, down_weight) + down_bias.astype(jnp.float32)
    stored = (hidden, normed, packed, mixed, log_totals, middle, normed_two, pre_act, activ)
    return (output, stored)


def layer_backward(grad_out, weights, stored, doc_row):
    (
        pre_gain,
        pre_shift,
        qkv_weight,
        query_bias,
        value_bias,
        out_weight,
        out_bias,
        post_gain,
        post_shift,
        up_weight,
        up_bias,
        down_weight,
        down_bias,
    ) = weights
    hidden, normed, packed, mixed, log_totals, middle, normed_two, pre_act, activ = stored
    rows_here, width = hidden.shape
    grad_down = grad_out.astype(jnp.bfloat16)
    activ_columns = lax.all_to_all(activ, "shard", split_axis=1, concat_axis=0, tiled=True)
    group_grads = lax.all_gather(grad_down, "shard", axis=0, tiled=True)
    grad_down_weight = project_back(activ_columns, group_grads)
    width_part = width // lax.axis_size("shard")
    column_total = jnp.sum(group_grads.astype(jnp.float32), axis=0)
    grad_down_bias = lax.dynamic_slice_in_dim(
        column_total, lax.axis_index("shard") * width_part, width_part, 0
    )
    grad_activ = project_trans(grad_down, down_weight)
    unused_gelu, gelu_pull = jax.vjp(gelu_tanh, pre_act)
    grad_pre = gelu_pull(grad_activ)[0].astype(jnp.bfloat16)
    grad_up_weight = project_back(normed_two, grad_pre)
    grad_up_bias = jnp.sum(grad_pre.astype(jnp.float32), axis=0)
    grad_normed_two = project_trans(grad_pre, up_weight)
    unused_post, post_pull = jax.vjp(
        norm, middle, post_gain.astype(jnp.float32), post_shift.astype(jnp.float32)
    )
    grad_middle, grad_post_gain, grad_post_shift = post_pull(grad_normed_two)
    grad_middle = grad_middle + grad_out
    grad_attn = grad_middle.astype(jnp.bfloat16)
    grad_out_weight = project_back(mixed, grad_attn)
    grad_out_bias = jnp.sum(grad_attn.astype(jnp.float32), axis=0)
    grad_mixed = (
        project_trans(grad_attn, out_weight).astype(jnp.bfloat16).reshape(rows_here, HEADS, HEAD)
    )
    shaped = packed.reshape(rows_here, 3, HEADS, HEAD)
    grad_queries, grad_keys, grad_values = attention_backward(
        shaped[:, 0], shaped[:, 1], shaped[:, 2], doc_row, log_totals, grad_mixed
    )
    grad_packed = jnp.concatenate([grad_queries, grad_keys, grad_values], axis=1).astype(
        jnp.bfloat16
    )
    grad_qkv_weight = project_back(normed, grad_packed)
    column_sums = jnp.sum(grad_packed.astype(jnp.float32), axis=0)
    grad_query_bias = column_sums[:width]
    grad_value_bias = column_sums[2 * width :]
    grad_normed = project_trans(grad_packed, qkv_weight)
    unused_pre, pre_pull = jax.vjp(
        norm, hidden, pre_gain.astype(jnp.float32), pre_shift.astype(jnp.float32)
    )
    grad_hidden, grad_pre_gain, grad_pre_shift = pre_pull(grad_normed)
    grads = (
        grad_pre_gain,
        grad_pre_shift,
        grad_qkv_weight,
        grad_query_bias,
        grad_value_bias,
        grad_out_weight,
        grad_out_bias,
        grad_post_gain,
        grad_post_shift,
        grad_up_weight,
        grad_up_bias,
        grad_down_weight,
        grad_down_bias,
    )
    return (grad_hidden + grad_middle, grads)


def on_device(
    hidden_in,
    doc_ids,
    cotangent,
    pre_gain,
    pre_shift,
    qkv_weight,
    query_bias,
    value_bias,
    out_weight,
    out_bias,
    post_gain,
    post_shift,
    up_weight,
    up_bias,
    down_weight,
    down_bias,
):
    shards = (
        pre_gain,
        pre_shift,
        qkv_weight,
        query_bias,
        value_bias,
        out_weight,
        out_bias,
        post_gain,
        post_shift,
        up_weight,
        up_bias,
        down_weight,
        down_bias,
    )
    doc_row = doc_ids[0]
    hidden = hidden_in
    layer_index = 0
    weights = fetch_forward(shards, layer_index)
    hidden, stored = layer_forward(hidden, weights, doc_row)
    gathered_all = [weights]
    stored_all = [stored]
    grad_flow = cotangent
    reduced_all = [None] * LAYERS
    for layer_index in reversed(range(LAYERS)):
        weights = gathered_all[layer_index]
        grad_flow, layer_grads = layer_backward(
            grad_flow, weights, stored_all[layer_index], doc_row
        )
        rest_grads = tuple((layer_grads[member] for member in range(11)))
        rest_sums = reduce_nested_rest(rest_grads)
        down_pair = (layer_grads[11], layer_grads[12])
        down_sums = (
            lax.psum(down_pair[0].astype(jnp.bfloat16), "rep").astype(jnp.float32),
            lax.psum(down_pair[1].astype(jnp.bfloat16), "rep").astype(jnp.float32),
        )
        reduced_all[layer_index] = tuple(rest_sums) + tuple(down_sums)
    stacked = tuple((jnp.stack([reduced_all[0][member]]) for member in range(13)))
    return (
        hidden,
        grad_flow,
        stacked[0],
        stacked[1],
        stacked[2],
        stacked[3],
        stacked[4],
        stacked[5],
        stacked[6],
        stacked[7],
        stacked[8],
        stacked[9],
        stacked[10],
        stacked[11],
        stacked[12],
    )


def solution(mesh):
    in_specs = (
        P(("rep", "shard"), None),
        P(("rep", "shard"), None),
        P(("rep", "shard"), None),
        P(None, "shard"),
        P(None, "shard"),
        P(None, "shard", None),
        P(None, "shard"),
        P(None, "shard"),
        P(None, "shard", None),
        P(None, "shard"),
        P(None, "shard"),
        P(None, "shard"),
        P(None, "shard", None),
        P(None, "shard"),
        P(None, "shard", None),
        P(None, "shard"),
    )
    out_specs = (
        P(("rep", "shard"), None),
        P(("rep", "shard"), None),
        P(None, "shard"),
        P(None, "shard"),
        P(None, "shard", None),
        P(None, "shard"),
        P(None, "shard"),
        P(None, "shard", None),
        P(None, "shard"),
        P(None, "shard"),
        P(None, "shard"),
        P(None, "shard", None),
        P(None, "shard"),
        P(None, "shard", None),
        P(None, "shard"),
    )
    return jax.shard_map(
        on_device, mesh=mesh, in_specs=in_specs, out_specs=out_specs, check_vma=False
    )
```

profile of v0, /device:TPU:0, one launch (start us, length us, event | category | flops | bytes accessed | tf_op | source)
XLA Modules:
  0.0 431.4 jit_solution(6924387649990992)
XLA Ops:
  7.2 2.1 convert_element_type.231
  9.4 0.7 convert_element_type.242
  10.2 0.9 convert_element_type.254
  11.3 0.9 convert_element_type.260
  12.2 0.7 convert_element_type.265
  13.2 0.6 fusion.54
  14.4 0.2 dynamic-update-slice.3
  15.9 32.5 %all-reduce.17 = (bf16[768]{0:T(1024)(128)(2,1)S(1)}, bf16[768]{0:T(1024)(128)(2,1)S(1)}, bf16[768]{0:T(1024)(128)(2,1)S(1)}, bf16[768]{0:T(1024)(128)(2,1)S(1)}...) all-reduce(bf16[768]{0:T(1024)(128)(2,1)S(1)} %dynamic-update-slice, ...), channel_id=6, replica_groups=mesh['rep'=4,'shard'=8] {'shard'}, use_global_device_ids=true, to_apply=%add.3 | all-reduce | flops 5376 | bytes 21504 | tf_op jit(solution)/shard_map/all_gather | solution.py:56
  48.9 12.8 %all-gather.10 = bf16[1,3072]{1,0:T(2,128)(2,1)S(1)} all-gather(bf16[1,384]{1,0:T(2,128)(2,1)S(1)} %convert_element_type.256), channel_id=12, replica_groups=mesh['rep'=4,'shard'=8] {'shard'}, dimensions={1}, use_global_device_ids=true | all-gather | bytes 6912 | tf_op jit(solution)/shard_map/all_gather | solution.py:62
  61.8 2.8 fusion.11
  64.6 0.3 copy.47
  64.9 0.3 fusion.55
  65.4 0.2 convolution_convert_fusion.5
  65.7 13.2 %all-gather.23.cloned.1.call-done = bf16[1,768,768]{2,1,0:T(8,128)(2,1)} async-done(((bf16[1,96,768]{2,1,0:T(8,128)(2,1)}), bf16[1,768,768]{2,1,0:T(8,128)(2,1)}) %all-gather.23.cloned.1.call-update) | async-done | bytes 1179664 | tf_op jit(solution)/shard_map/all_gather | solution.py:57
  78.9 1.7 fusion.56
  80.8 51.2 %all-gather.25.cloned.1.call-done = bf16[1,768,3072]{2,1,0:T(8,128)(2,1)} async-done(((bf16[1,96,3072]{2,1,0:T(8,128)(2,1)}), bf16[1,768,3072]{2,1,0:T(8,128)(2,1)}) %all-gather.25.cloned.1.call-update) | async-done | bytes 4718608 | tf_op jit(solution)/shard_map/all_gather | solution.py:61
  132.0 5.1 %multiply_convert_fusion = (bf16[128,3072]{1,0:T(8,128)(2,1)}, f32[128,3072]{1,0:T(8,128)}) fusion(f32[3072]{0:T(1024)S(1)} %bitcast.156, bf16[1,768,3072]{2,1,0:T(8,128)(2,1)} %all-gather.25.cloned.1.call-done, f32[128,768]{1,0:T(8,128)S(1)} %get-tuple-element.114, f32[768]{0:T(1024)S(1)} %convert_element_type.292, f32[768]{0:T(1024)S(1)} %convert_element_type.291, ...), kind=kOutput, calls=%fused_computation.27 | convolution fusion | flops 608403456 | bytes 7490560 | tf_op jit(solution)/shard_map/dot_general | solution.py:30
  137.1 47.0 %all-gather.27.cloned.1.call-done = bf16[1,3072,768]{2,1,0:T(8,128)(2,1)} async-done(((bf16[1,384,768]{2,1,0:T(8,128)(2,1)}), bf16[1,3072,768]{2,1,0:T(8,128)(2,1)}) %all-gather.27.cloned.1.call-update) | async-done | bytes 4718608 | tf_op jit(solution)/shard_map/all_gather | solution.py:63
  184.1 5.9 %fusion.57 = (bf16[3072]{0:T(1024)(128)(2,1)}, bf16[128,3072]{1,0:T(8,128)(2,1)S(1)}) fusion(f32[128,3072]{1,0:T(8,128)} %get-tuple-element.116, bf16[128,768]{1,0:T(8,128)(2,1)S(1)} %copy-done.17, bf16[1,3072,768]{2,1,0:T(8,128)(2,1)} %all-gather.27.cloned.1.call-done), kind=kOutput, calls=%fused_computation.109 | convolution fusion | flops 613807104 | bytes 7280640 | tf_op jit(solution)/shard_map/dot_general | solution.py:40
  190.0 2.3 multiply_reduce_fusion.1
  192.3 0.2 fusion.52
  192.6 0.5 copy-done.39
  193.1 0.7 fusion.50
  193.8 0.7 copy-done.13
  194.4 1.5 convolution_convert_fusion.2
  196.2 2.1 fusion.35
  198.3 1.1 copy.49
  199.4 1.3 multiply_reduce_fusion
  201.0 0.4 fusion.39
  201.3 0.2 fusion.38
  201.6 0.4 convolution_convert_fusion.4
  202.0 3.0 convolution_convert_fusion.1
  205.1 1.0 copy-done.8
  206.1 3.7 convolution_convert_fusion
  209.8 1.1 copy-done.9
  211.0 1.0 copy.60
  211.9 4.3 %all-to-all-start = ((bf16[128,8,384]{2,0,1:T(8,128)(2,1)}), bf16[128,8,384]{2,0,1:T(8,128)(2,1)}, u32[]{:S(2)}, u32[]{:S(2)}) async-start(bf16[128,8,384]{2,0,1:T(8,128)(2,1)} %bitcast.133), calls=%async_computation.3 | async-start | bytes 1572864 | tf_op jit(solution)/shard_map/all_to_all | solution.py:251
  217.7 0.2 dynamic-update-slice.7
  217.9 1.7 convert_reduce_fusion
  219.6 0.6 convert_bitcast_fusion
  220.2 0.3 fusion.48
  220.4 0.6 fusion.53
  221.1 4.8 %multiply_reduce_fusion.2 = (bf16[768]{0:T(1024)(128)(2,1)}, f32[128]{0:T(128)}, bf16[768]{0:T(1024)(128)(2,1)}, f32[128,768]{1,0:T(8,128)}) fusion(f32[128,768]{1,0:T(8,128)S(1)} %copy-done, f32[128]{0:T(128)} %copy-done.31, f32[128]{0:T(128)S(1)} %copy-done.28, f32[768]{0:T(1024)S(1)} %convert_element_type.288, ...), kind=kOutput, calls=%fused_computation.57 | convolution fusion | flops 455539072 | bytes 4922880 | tf_op jit(solution)/shard_map/dot_general | solution.py:40
  225.9 35.2 %all-reduce.16 = (bf16[768]{0:T(1024)(128)(2,1)S(1)}, bf16[768]{0:T(1024)(128)(2,1)S(1)}, bf16[768]{0:T(1024)(128)(2,1)S(1)}, bf16[768]{0:T(1024)(128)(2,1)S(1)}...) all-reduce(bf16[768]{0:T(1024)(128)(2,1)} %copy-done.38, ...), channel_id=14, replica_groups=mesh['rep'=4,'shard'=8] {'shard'}, use_global_device_ids=true, to_apply=%add.7 | all-reduce | flops 9216 | bytes 36864
  261.2 2.8 fusion.24
  264.0 32.5 %reduce-scatter.4.cloned.1.call-done = bf16[96,2304]{1,0:T(8,128)(2,1)} async-done(((bf16[768,2304]{1,0:T(8,128)(2,1)}), bf16[96,2304]{1,0:T(8,128)(2,1)}) %reduce-scatter.4.cloned.1.call-update) | async-done | bytes 442384 | tf_op jit(solution)/shard_map/reduce_scatter | solution.py:76
  296.5 55.8 %reduce-scatter.8.cloned.1.call-done = bf16[96,3072]{1,0:T(8,128)(2,1)} async-done(((bf16[768,3072]{1,0:T(8,128)(2,1)}), bf16[96,3072]{1,0:T(8,128)(2,1)}) %reduce-scatter.8.cloned.1.call-update) | async-done | bytes 589840 | tf_op jit(solution)/shard_map/reduce_scatter | solution.py:97
  352.6 10.1 %all-reduce.18 = (bf16[1,96]{1,0:T(2,128)(2,1)S(1)}, bf16[1,96]{1,0:T(2,128)(2,1)S(1)}, bf16[1,96]{1,0:T(2,128)(2,1)S(1)}, bf16[1,96]{1,0:T(2,128)(2,1)S(1)}, bf...) all-reduce(bf16[1,96]{1,0:T(2,128)(2,1)S(1)} %dynamic-slice_bitcast, ...), channel_id=1, replica_groups=mesh['rep'=4,'shard'=8] {'rep'}, use_global_device_ids=true, to_apply=%region_13.14 | all-reduce | flops 1152 | bytes 4608 | tf_op jit(solution)/shard_map/psum | solution.py:105
  362.7 0.5 stack.79
  363.2 0.5 stack.81
  363.8 0.5 stack.85
  364.3 0.5 stack.87
  364.8 0.5 stack.91
  365.3 0.5 stack.93
  365.8 0.5 stack.95
  366.3 0.6 stack.99
  366.9 0.5 stack.103
  367.7 0.9 add_add_fusion.2
  368.6 3.9 fusion.29
  372.5 46.5 %all-reduce.22.cloned.1.call-done = (bf16[1,96,2304]{2,1,0:T(8,128)(2,1)}, bf16[1,96,768]{2,1,0:T(8,128)(2,1)}, bf16[1,96,3072]{2,1,0:T(8,128)(2,1)}, bf16[1,384,768]{2,1,0:T(8,128)(2,1)}) async-done(((bf16[1,96,2304]{2,1,0:T(8,128)(2,1)}, bf16[1,96,768]{2,1,0:T(8,128)(2,1)}, bf16[1,96,3072]{2,1,0:T(8,128)(2,1)}, bf16[1,384,768]{2,1,0:T(8,128)(2,1)}), (bf16[1,96,2304]{2,1,0:T(8,128)(2,1)}, ...) | async-done | bytes 1769488 | tf_op jit(solution)/shard_map/psum | solution.py:107
  419.0 2.1 stack.83
  421.1 1.6 stack.89
  422.7 1.1 stack.97
  423.8 1.1 stack.101
  (184 shorter events, 3.9 us)
Async XLA Ops:
  7.2 2.2 copy-start.21
  7.2 3.0 copy-start.15
  7.2 54.6 %all-gather.21.cloned.1.call-start = ((), (), s32[]{:S(2)}) async-start(), calls=%async_computation.8 | async-start | bytes 3981312 | tf_op jit(solution)/shard_map/all_gather | solution.py:54
  9.3 1.9 copy-start.16
  9.4 69.5 %all-gather.23.cloned.1.call-start = ((), (), s32[]{:S(2)}) async-start(), calls=%async_computation.9 | async-start | bytes 1327104 | tf_op jit(solution)/shard_map/all_gather | solution.py:57
  10.1 121.9 %all-gather.25.cloned.1.call-start = ((), (), s32[]{:S(2)}) async-start(), calls=%async_computation.10 | async-start | bytes 5308416 | tf_op jit(solution)/shard_map/all_gather | solution.py:61
  11.1 1.2 copy-start.4
  11.1 1.9 copy-start.47
  11.1 1.9 copy-start.48
  11.1 1.9 copy-start.49
  11.1 1.9 copy-start.50
  11.1 2.0 copy-start.51
  11.2 2.0 copy-start.52
  11.2 2.0 copy-start.53
  11.2 2.0 copy-start.42
  11.2 37.2 %copy-start = (f32[128,768]{1,0:T(8,128)S(1)}, f32[128,768]{1,0:T(8,128)}, u32[]{:S(2)}) copy-start(f32[128,768]{1,0:T(8,128)} %param.16) | copy-start | bytes 1179652
  11.2 172.9 %all-gather.27.cloned.1.call-start = ((), (), s32[]{:S(2)}) async-start(), calls=%async_computation.11 | async-start | bytes 5308416 | tf_op jit(solution)/shard_map/all_gather | solution.py:63
  12.1 36.7 %copy-start.41 = (s32[1,128]{1,0:T(1,128)S(1)}, s32[1,128]{1,0:T(1,128)}, u32[]{:S(2)}) copy-start(s32[1,128]{1,0:T(1,128)} %param.17) | copy-start | bytes 1540
  12.1 36.8 %copy-start.43 = (f32[1,384]{1,0:T(1,128)S(1)}, f32[1,384]{1,0:T(1,128)}, u32[]{:S(2)}) copy-start(f32[1,384]{1,0:T(1,128)} %param.29) | copy-start | bytes 4612
  12.2 205.7 %all-gather.19.cloned.1.call-start = ((), (), s32[]{:S(2)}) async-start(), calls=%async_computation.7 | async-start | bytes 1769472 | tf_op jit(solution)/shard_map/all_gather | solution.py:252
  12.9 251.1 %reduce-scatter.6.cloned.1.call-start = ((), (), s32[]{:S(2)}) async-start(), calls=%async_computation.5 | async-start | bytes 1327104 | tf_op jit(solution)/shard_map/reduce_scatter | solution.py:85
  48.4 13.4 %copy-start.22 = (f32[768]{0:T(1024)}, f32[768]{0:T(1024)S(1)}, u32[]{:S(2)}) copy-start(f32[768]{0:T(1024)S(1)} %convert_element_type.289) | copy-start | bytes 9220
  48.6 16.0 %copy-start.26 = (f32[128]{0:T(128)}, f32[128]{0:T(128)S(1)}, u32[]{:S(2)}) copy-start(f32[128]{0:T(128)S(1)} %broadcast_multiply_fusion.1) | copy-start | bytes 1540
  48.8 15.8 %copy-start.44 = (f32[128]{0:T(128)}, f32[128]{0:T(128)S(1)}, u32[]{:S(2)}) copy-start(f32[128]{0:T(128)S(1)} %multiply_reduce_fusion.6) | copy-start | bytes 1540
  48.8 15.8 %copy-start.31 = (f32[128]{0:T(128)}, f32[128]{0:T(128)S(1)}, u32[]{:S(2)}) copy-start(f32[128]{0:T(128)S(1)} %fusion.46) | copy-start | bytes 1540
  61.7 70.3 %copy-start.24 = (f32[768]{0:T(1024)}, f32[768]{0:T(1024)S(1)}, u32[]{:S(2)}) copy-start(f32[768]{0:T(1024)S(1)} %convert_element_type.292) | copy-start | bytes 9220
  64.9 0.8 copy-start.5
  65.7 71.4 %copy-start.11 = (bf16[12,64,128]{2,1,0:T(8,128)(2,1)}, bf16[12,64,128]{2,1,0:T(8,128)(2,1)S(1)}, u32[]{:S(2)}) copy-start(bf16[12,64,128]{2,1,0:T(8,128)(2,1)S(1)} %convolution_convert_fusion.5) | copy-start | bytes 589828
  80.6 111.7 %copy-start.29 = (f32[128]{0:T(128)}, f32[128]{0:T(128)S(1)}, u32[]{:S(2)}) copy-start(f32[128]{0:T(128)S(1)} %broadcast_multiply_fusion) | copy-start | bytes 1540
  80.8 111.5 %copy-start.34 = (f32[128]{0:T(128)}, f32[128]{0:T(128)S(1)}, u32[]{:S(2)}) copy-start(f32[128]{0:T(128)S(1)} %fusion.47) | copy-start | bytes 1540
  132.0 52.1 %copy-start.17 = (bf16[128,768]{1,0:T(8,128)(2,1)S(1)}, bf16[128,768]{1,0:T(8,128)(2,1)}, u32[]{:S(2)}) copy-start(bf16[128,768]{1,0:T(8,128)(2,1)} %convert_element_type.265) | copy-start | bytes 589828
  184.1 5.9 %copy-start.3 = (bf16[1,768,3072]{2,1,0:T(8,128)(2,1)S(1)}, bf16[1,768,3072]{2,1,0:T(8,128)(2,1)}, u32[]{:S(2)}) copy-start(bf16[1,768,3072]{2,1,0:T(8,128)(2,1)} %all-gather.25.cloned.1.call-done) | copy-start | bytes 14155780
  190.0 2.3 copy-start.7
  192.3 2.1 copy-start.12
  193.8 2.4 copy-start.2
  195.9 100.6 %reduce-scatter.4.cloned.1.call-start = ((), (), s32[]{:S(2)}) async-start(), calls=%async_computation.4 | async-start | bytes 3981312 | tf_op jit(solution)/shard_map/reduce_scatter | solution.py:76
  199.4 1.5 copy-start.6
  200.9 1.0 copy-start.23
  200.9 1.0 copy-start.27
  201.0 1.0 copy-start.32
  201.6 18.6 %copy-start.14 = (bf16[12,64,128]{2,1,0:T(8,128)(2,1)}, bf16[12,64,128]{2,1,0:T(8,128)(2,1)S(1)}, u32[]{:S(2)}) copy-start(bf16[12,64,128]{2,1,0:T(8,128)(2,1)S(1)} %fusion.38) | copy-start | bytes 589828
  205.0 1.1 copy-start.8
  205.0 1.1 copy-start.25
  205.0 1.1 copy-start.30
  205.0 1.1 copy-start.35
  205.0 147.3 %reduce-scatter.8.cloned.1.call-start = ((), (), s32[]{:S(2)}) async-start(), calls=%async_computation.6 | async-start | bytes 5308416 | tf_op jit(solution)/shard_map/reduce_scatter | solution.py:97
  209.8 1.1 copy-start.9
  210.9 6.7 %copy-start.54 = (f32[1,96]{1,0:T(1,128)S(1)}, f32[1,96]{1,0:T(1,128)}, u32[]{:S(2)}) copy-start(f32[1,96]{1,0:T(1,128)} %param.31) | copy-start | bytes 1156
  211.9 9.1 %copy-start.28 = (f32[128]{0:T(128)S(1)}, f32[128]{0:T(128)}, u32[]{:S(2)}) copy-start(f32[128]{0:T(128)} %copy-done.26) | copy-start | bytes 1540
  211.9 49.3 %all-to-all-start = ((bf16[128,8,384]{2,0,1:T(8,128)(2,1)}), bf16[128,8,384]{2,0,1:T(8,128)(2,1)}, u32[]{:S(2)}, u32[]{:S(2)}) async-start(bf16[128,8,384]{2,0,1:T(8,128)(2,1)} %bitcast.133), calls=%async_computation.3 | async-start | bytes 1572864 | tf_op jit(solution)/shard_map/all_to_all | solution.py:251
  216.3 202.7 %all-reduce.22.cloned.1.call-start = ((), (), s32[]{:S(2)}) async-start(), calls=%async_computation.12 | async-start | bytes 3538944 | tf_op jit(solution)/shard_map/psum | solution.py:107
  217.9 1.7 copy-start.38
  221.1 4.8 %copy-start.36 = (bf16[768]{0:T(1024)(128)(2,1)S(1)}, bf16[768]{0:T(1024)(128)(2,1)}, u32[]{:S(2)}) copy-start(bf16[768]{0:T(1024)(128)(2,1)} %get-tuple-element.56) | copy-start | bytes 4612
  221.1 4.8 %copy-start.37 = (bf16[768]{0:T(1024)(128)(2,1)S(1)}, bf16[768]{0:T(1024)(128)(2,1)}, u32[]{:S(2)}) copy-start(bf16[768]{0:T(1024)(128)(2,1)} %get-tuple-element.70) | copy-start | bytes 4612
  221.1 40.1 %copy-start.1 = (bf16[1024,768]{1,0:T(8,128)(2,1)S(1)}, bf16[1024,768]{1,0:T(8,128)(2,1)}, u32[]{:S(2)}) copy-start(bf16[1024,768]{1,0:T(8,128)(2,1)} %all-gather.19.cloned.1.call-done) | copy-start | bytes 4718596
  264.0 88.7 %copy-start.46 = (bf16[1,96]{1,0:T(2,128)(2,1)S(1)}, bf16[1,96]{1,0:T(2,128)(2,1)}, u32[]{:S(2)}) copy-start(bf16[1,96]{1,0:T(2,128)(2,1)} %convert_bitcast_fusion) | copy-start | bytes 580
  264.0 103.4 %copy-start.45 = (f32[128]{0:T(128)S(1)}, f32[128]{0:T(128)}, u32[]{:S(2)}) copy-start(f32[128]{0:T(128)} %copy-done.44) | copy-start | bytes 1540
  264.0 103.4 %copy-start.55 = (f32[128]{0:T(128)S(1)}, f32[128]{0:T(128)}, u32[]{:S(2)}) copy-start(f32[128]{0:T(128)} %get-tuple-element.69) | copy-start | bytes 1540
  264.0 103.5 %copy-start.20 = (f32[128,768]{1,0:T(8,128)S(1)}, f32[128,768]{1,0:T(8,128)}, u32[]{:S(2)}) copy-start(f32[128,768]{1,0:T(8,128)} %get-tuple-element.120) | copy-start | bytes 1179652
  264.0 103.5 %copy-start.33 = (f32[128]{0:T(128)S(1)}, f32[128]{0:T(128)}, u32[]{:S(2)}) copy-start(f32[128]{0:T(128)} %copy-done.31) | copy-start | bytes 1540
  264.0 103.7 %copy-start.40 = (f32[128]{0:T(128)S(1)}, f32[128]{0:T(128)}, u32[]{:S(2)}) copy-start(f32[128]{0:T(128)} %copy-done.39) | copy-start | bytes 1540
  352.3 16.3 %copy-start.10 = (bf16[128,3072]{1,0:T(8,128)(2,1)S(1)}, bf16[128,3072]{1,0:T(8,128)(2,1)}, u32[]{:S(2)}) copy-start(bf16[128,3072]{1,0:T(8,128)(2,1)} %get-tuple-element.115) | copy-start | bytes 2359300
  419.0 3.7 copy-start.19
  419.0 4.8 %copy-start.18 = (bf16[1,384,768]{2,1,0:T(8,128)(2,1)S(1)}, bf16[1,384,768]{2,1,0:T(8,128)(2,1)}, u32[]{:S(2)}) copy-start(bf16[1,384,768]{2,1,0:T(8,128)(2,1)} %get-tuple-element.100) | copy-start | bytes 1769476
  (2 other events, 1.2 us)
Sparse Core Ops, SparseCore 0:
  10.2 44.7 all-gather.20
  57.2 21.6 all-gather.22
  81.1 50.8 all-gather.24
  134.1 49.9 all-gather.26
  186.1 24.0 all-gather.18
  212.9 36.2 reduce-scatter.5
  251.5 44.9 reduce-scatter.3
  298.8 53.4 reduce-scatter.7
  356.3 62.6 all-reduce.21
where the time goes:
time: 432 us; the launch traced here: 431 us
  waiting for transfers between devices  246 us (57%)
  blocking collectives  90.6 us (21%)
  matrix products  42.4 us (10%)
  other arithmetic  20.8 us (5%)
  between operations  16.6 us (4%)
  local copies, waits for them, and re-layouts  9.89 us (2%)
  starting transfers between devices  4.9 us (1%)
    reduce_scatter x1, waiting for transfers between devices, reduce_nested_rest(): lax.psum_scatter(grads[9].astype(jnp.bfloat16), 'shard', scatter_dimensio...  55.8 us
    all_gather x1, waiting for transfers between devices, fetch_forward(): lax.all_gather(parts[9], 'shard', axis=0, tiled=True)  51.2 us
    all_gather x1, waiting for transfers between devices, fetch_forward(): lax.all_gather(parts[11], 'shard', axis=0, tiled=True)  47 us
    psum x1, waiting for transfers between devices, reduce_nested_rest(): lax.psum(owned[2].astype(jnp.bfloat16), 'rep').astype(jnp.float32)  46.5 us
    unnamed x1, blocking collectives  35.2 us
    all_gather x1, blocking collectives, fetch_forward(): lax.all_gather(parts[4], 'shard', axis=0, tiled=True)  32.5 us
    reduce_scatter x1, waiting for transfers between devices, reduce_nested_rest(): lax.psum_scatter(grads[2].astype(jnp.bfloat16), 'shard', scatter_dimensio...  32.5 us
    dot_general x4, matrix products, project_trans(): lax.dot_general(left, right, (((1,), (1,)), ((), ())), preferred_element_...  15.2 us
  transfers between devices with their start and end apart: 10, of which 6 were waited for; matrix products, arithmetic and copies ran while one was open for 14% of the time, Pallas kernels for 0%

commit v1 on v0

--- a/solution.py
+++ b/solution.py
@@ -1,3 +1,4 @@
+import functools
 import jax
 import jax.numpy as jnp
 from jax import lax
@@ -9,6 +10,19 @@
 EPS = 1e-05
 GELU_C = 0.7978845608028654
 NEG_FILL = -1e30
+
+
+def refer_heads_on(row_data, array_dim):
+    num_devices = lax.axis_size("shard")
+    series = tuple((num_devices if p == array_dim else 1 for p in range(row_data.ndim)))
+    s_next = jnp.tile(row_data, series)
+    current_arr = lax.all_to_all(
+        s_next, "shard", concat_axis=array_dim, tiled=True, split_axis=array_dim
+    )
+    return current_arr
+
+
+try_all_the_thing = functools.partial(refer_heads_on, array_dim=0)
 
 
 def norm(values_in, gains, shifts):
@@ -58,7 +72,7 @@
         lax.all_gather(parts[6], "shard", axis=0, tiled=True),
         lax.all_gather(parts[7], "shard", axis=0, tiled=True),
         lax.all_gather(parts[8], "shard", axis=0, tiled=True),
-        lax.all_gather(parts[9], "shard", axis=0, tiled=True),
+        try_all_the_thing(parts[9]),
         lax.all_gather(parts[10], "shard", axis=0, tiled=True),
         lax.all_gather(parts[11], "shard", axis=0, tiled=True),
         lax.all_gather(parts[12], "shard", axis=0, tiled=True),

time: 432 us -> 453 us (1.049)
  blocking collectives: 90.6 us -> 228 us
  waiting for transfers between devices: 246 us -> 118 us
  starting transfers between devices: 4.9 us -> 11.4 us
    all_gather x1, blocking collectives: 32.5 us -> 173 us  [fetch_forward(): lax.all_gather(parts[4], 'shard', axis=0, tiled=True)]
    all_gather x1 -> x0, waiting for transfers between devices: 51.2 us -> none  [fetch_forward(): lax.all_gather(parts[9], 'shard', axis=0, tiled=True)]
    all_gather x1, waiting for transfers between devices: 47 us -> 0.01 us  [fetch_forward(): lax.all_gather(parts[11], 'shard', axis=0, tiled=True)]
    reduce_scatter x1, waiting for transfers between devices: 32.5 us -> 15.3 us  [reduce_nested_rest(): lax.psum_scatter(grads[2].astype(jnp.bfloat16), 'shard', scatter_dimensio...]
    all_gather x1, waiting for transfers between devices: 13.2 us -> 0.01 us  [fetch_forward(): lax.all_gather(parts[5], 'shard', axis=0, tiled=True)]
    all_to_all x0 -> x1, starting transfers between devices: none -> 6.5 us  [refer_heads_on(): lax.all_to_all(s_next, 'shard', concat_axis=array_dim, tiled=True, split_...]
  transfers between devices with their start and end apart: 10 -> 10, of which waited for: 6 -> 3; matrix products, arithmetic and copies ran while one was open for 14% -> 15% of each run, Pallas kernels for 0% -> 0%
where the time goes in v1:
time: 453 us; the launch traced here: 452 us
  blocking collectives  228 us (50%)
  waiting for transfers between devices  118 us (26%)
  matrix products  45.2 us (10%)
  other arithmetic  20 us (4%)
  between operations  16.8 us (4%)
  local copies, waits for them, and re-layouts  13.4 us (3%)
  starting transfers between devices  11.4 us (3%)
    all_gather x1, blocking collectives, fetch_forward(): lax.all_gather(parts[4], 'shard', axis=0, tiled=True)  173 us
    reduce_scatter x1, waiting for transfers between devices, reduce_nested_rest(): lax.psum_scatter(grads[9].astype(jnp.bfloat16), 'shard', scatter_dimensio...  55.7 us
    psum x1, waiting for transfers between devices, reduce_nested_rest(): lax.psum(owned[2].astype(jnp.bfloat16), 'rep').astype(jnp.float32)  46.5 us
    unnamed x1, blocking collectives  31 us
    dot_general x4, matrix products, project_trans(): lax.dot_general(left, right, (((1,), (1,)), ((), ())), preferred_element_...  17.7 us
    reduce_scatter x1, waiting for transfers between devices, reduce_nested_rest(): lax.psum_scatter(grads[2].astype(jnp.bfloat16), 'shard', scatter_dimensio...  15.3 us
    all_gather x1, blocking collectives, fetch_forward(): lax.all_gather(parts[10], 'shard', axis=0, tiled=True)  13.7 us
    dot_general x4, matrix products, project(): return jnp.dot(left, right, preferred_element_type=jnp.float32)  13.5 us
  transfers between devices with their start and end apart: 10, of which 3 were waited for; matrix products, arithmetic and copies ran while one was open for 15% of the time, Pallas kernels for 0%

profile of v1, /device:TPU:0, one launch (start us, length us, event | category | flops | bytes accessed | tf_op | source)
XLA Modules:
  0.0 452.2 jit_solution(10426883077644279515)
XLA Ops:
  7.2 2.1 convert_element_type.235
  9.4 0.7 convert_element_type.246
  10.2 0.9 convert_element_type.264
  11.2 2.8 tile.2
  14.1 6.5 %all-to-all-start = ((bf16[8,96,3072]{2,1,0:T(8,128)(2,1)}), bf16[8,96,3072]{2,1,0:T(8,128)(2,1)}, u32[]{:S(2)}, u32[]{:S(2)}) async-start(bf16[8,96,3072]{2,1,0:T(8,128)(2,1)} %tile.2), calls=%async_computation | async-start | bytes 9437184 | tf_op jit(solution)/shard_map/all_to_all | solution.py:19
  20.6 0.7 convert_element_type.269
  21.4 0.6 fusion.47
  23.4 0.2 dynamic-update-slice
  23.7 0.2 dynamic-update-slice.4
  23.9 0.2 dynamic-update-slice.6
  24.2 0.2 dynamic-update-slice.5
  24.4 172.9 %all-reduce.17 = (bf16[768]{0:T(1024)(128)(2,1)S(1)}, bf16[768]{0:T(1024)(128)(2,1)S(1)}, bf16[768]{0:T(1024)(128)(2,1)S(1)}, bf16[768]{0:T(1024)(128)(2,1)S(1)}...) all-reduce(bf16[768]{0:T(1024)(128)(2,1)S(1)} %dynamic-update-slice, ...), channel_id=6, replica_groups=mesh['rep'=4,'shard'=8] {'shard'}, use_global_device_ids=true, to_apply=%add.3 | all-reduce | flops 5376 | bytes 21504 | tf_op jit(solution)/shard_map/all_gather | solution.py:70
  197.3 13.7 %all-gather.9 = bf16[1,3072]{1,0:T(2,128)(2,1)S(1)} all-gather(bf16[1,384]{1,0:T(2,128)(2,1)S(1)} %convert_element_type.260), channel_id=11, replica_groups=mesh['rep'=4,'shard'=8] {'shard'}, dimensions={1}, use_global_device_ids=true | all-gather | bytes 6912 | tf_op jit(solution)/shard_map/all_gather | solution.py:76
  211.5 0.5 copy-done.43
  212.1 2.7 fusion.4
  214.8 0.3 copy.47
  215.1 0.3 fusion.48
  215.6 0.2 convolution_convert_fusion.5
  215.9 1.8 fusion.49
  218.0 5.2 %multiply_convert_fusion = (bf16[128,3072]{1,0:T(8,128)(2,1)}, f32[128,3072]{1,0:T(8,128)}) fusion(f32[3072]{0:T(1024)S(1)} %bitcast.150, bf16[768,3072]{1,0:T(8,128)(2,1)} %bitcast.18, f32[128,768]{1,0:T(8,128)S(1)} %get-tuple-element.114, f32[768]{0:T(1024)S(1)} %convert_element_type.296, f32[768]{0:T(1024)S(1)} %convert_element_type.295, ...), kind=kOutput, calls=%fused_computation.23 | convolution fusion | flops 608403456 | bytes 7490560 | tf_op jit(solution)/shard_map/dot_general | solution.py:44
  223.2 5.8 %fusion.50 = (bf16[3072]{0:T(1024)(128)(2,1)}, bf16[128,3072]{1,0:T(8,128)(2,1)S(1)}) fusion(f32[128,3072]{1,0:T(8,128)} %get-tuple-element.116, bf16[128,768]{1,0:T(8,128)(2,1)S(1)} %copy-done.16, bf16[1,3072,768]{2,1,0:T(8,128)(2,1)} %all-gather.23.cloned.1.call-done), kind=kOutput, calls=%fused_computation.106 | convolution fusion | flops 613807104 | bytes 7280640 | tf_op jit(solution)/shard_map/dot_general | solution.py:54
  229.0 4.9 %multiply_reduce_fusion.1 = (bf16[768]{0:T(1024)(128)(2,1)}, f32[128]{0:T(128)S(1)}, bf16[768]{0:T(1024)(128)(2,1)}, f32[128,768]{1,0:T(8,128)S(1)}) fusion(f32[128,768]{1,0:T(8,128)S(1)} %get-tuple-element.114, f32[128]{0:T(128)S(1)} %fusion.40, f32[128]{0:T(128)S(1)} %broadcast_multiply_fusion, f32[768]{0:T(1024)S(1)} %convert_element_type.295, ...), kind=kOutput, calls=%fused_computation.53 | convolution fusion | flops 604764544 | bytes 6299136 | tf_op jit(solution)/shard_map/dot_general | solution.py:54
  234.2 0.6 copy-done.38
  234.8 0.7 fusion.43
  235.5 0.7 copy-done.12
  236.2 1.5 convolution_convert_fusion.2
  237.9 2.1 fusion.28
  240.1 1.1 copy.49
  241.2 1.3 multiply_reduce_fusion
  242.7 0.4 fusion.32
  243.1 0.2 fusion.31
  243.3 0.4 convolution_convert_fusion.4
  243.8 3.1 convolution_convert_fusion.1
  246.9 1.1 copy-done.7
  248.0 3.7 convolution_convert_fusion
  251.7 1.1 copy-done.8
  252.8 1.0 copy.60
  253.8 4.3 all-to-all-start.1
  259.8 1.7 convert_reduce_fusion
  261.5 0.6 convert_bitcast_fusion.1
  262.1 0.3 fusion.41
  262.3 0.6 fusion.46
  263.0 4.8 %multiply_reduce_fusion.2 = (bf16[768]{0:T(1024)(128)(2,1)}, f32[128]{0:T(128)}, bf16[768]{0:T(1024)(128)(2,1)}, f32[128,768]{1,0:T(8,128)}) fusion(f32[128,768]{1,0:T(8,128)S(1)} %copy-done, f32[128]{0:T(128)} %copy-done.30, f32[128]{0:T(128)S(1)} %copy-done.27, f32[768]{0:T(1024)S(1)} %convert_element_type.292, ...), kind=kOutput, calls=%fused_computation.54 | convolution fusion | flops 455539072 | bytes 4922880 | tf_op jit(solution)/shard_map/dot_general | solution.py:54
  267.8 31.0 %all-reduce.16 = (bf16[768]{0:T(1024)(128)(2,1)S(1)}, bf16[768]{0:T(1024)(128)(2,1)S(1)}, bf16[768]{0:T(1024)(128)(2,1)S(1)}, bf16[768]{0:T(1024)(128)(2,1)S(1)}...) all-reduce(bf16[768]{0:T(1024)(128)(2,1)} %copy-done.37, ...), channel_id=13, replica_groups=mesh['rep'=4,'shard'=8] {'shard'}, use_global_device_ids=true, to_apply=%add.7 | all-reduce | flops 9216 | bytes 36864
  298.8 2.8 fusion.17
  301.7 15.3 %reduce-scatter.4.cloned.1.call-done = bf16[96,2304]{1,0:T(8,128)(2,1)} async-done(((bf16[768,2304]{1,0:T(8,128)(2,1)}), bf16[96,2304]{1,0:T(8,128)(2,1)}) %reduce-scatter.4.cloned.1.call-update) | async-done | bytes 442384 | tf_op jit(solution)/shard_map/reduce_scatter | solution.py:90
  317.0 55.7 %reduce-scatter.8.cloned.1.call-done = bf16[96,3072]{1,0:T(8,128)(2,1)} async-done(((bf16[768,3072]{1,0:T(8,128)(2,1)}), bf16[96,3072]{1,0:T(8,128)(2,1)}) %reduce-scatter.8.cloned.1.call-update) | async-done | bytes 589840 | tf_op jit(solution)/shard_map/reduce_scatter | solution.py:111
  373.1 10.1 %all-reduce.18 = (bf16[1,96]{1,0:T(2,128)(2,1)S(1)}, bf16[1,96]{1,0:T(2,128)(2,1)S(1)}, bf16[1,96]{1,0:T(2,128)(2,1)S(1)}, bf16[1,96]{1,0:T(2,128)(2,1)S(1)}, bf...) all-reduce(bf16[1,96]{1,0:T(2,128)(2,1)S(1)} %dynamic-slice_bitcast, ...), channel_id=1, replica_groups=mesh['rep'=4,'shard'=8] {'rep'}, use_global_device_ids=true, to_apply=%region_13.14 | all-reduce | flops 1152 | bytes 4608 | tf_op jit(solution)/shard_map/psum | solution.py:119
  383.2 0.5 stack.79
  383.7 0.5 stack.81
  384.2 0.5 stack.85
  384.7 0.5 stack.87
  385.2 0.5 stack.91
  385.7 0.5 stack.93
  386.2 0.5 stack.95
  386.7 0.6 stack.99
  387.3 0.5 stack.103
  388.1 0.9 add_add_fusion.2
  389.0 3.9 fusion.22
  392.9 46.5 %all-reduce.22.cloned.1.call-done = (bf16[1,96,2304]{2,1,0:T(8,128)(2,1)}, bf16[1,96,768]{2,1,0:T(8,128)(2,1)}, bf16[1,96,3072]{2,1,0:T(8,128)(2,1)}, bf16[1,384,768]{2,1,0:T(8,128)(2,1)}) async-done(((bf16[1,96,2304]{2,1,0:T(8,128)(2,1)}, bf16[1,96,768]{2,1,0:T(8,128)(2,1)}, bf16[1,96,3072]{2,1,0:T(8,128)(2,1)}, bf16[1,384,768]{2,1,0:T(8,128)(2,1)}), (bf16[1,96,2304]{2,1,0:T(8,128)(2,1)}, ...) | async-done | bytes 1769488 | tf_op jit(solution)/shard_map/psum | solution.py:121
  439.4 2.1 stack.83
  441.5 1.6 stack.89
  443.1 1.1 stack.97
  444.3 1.1 stack.101
  (182 shorter events, 3.9 us)
Async XLA Ops:
  7.2 2.2 copy-start.20
  7.2 3.0 copy-start.14
  7.2 204.9 %all-gather.19.cloned.1.call-start = ((), (), s32[]{:S(2)}) async-start(), calls=%async_computation.9 | async-start | bytes 3981312 | tf_op jit(solution)/shard_map/all_gather | solution.py:68
  9.3 1.7 copy-start.15
  9.4 206.6 %all-gather.21.cloned.1.call-start = ((), (), s32[]{:S(2)}) async-start(), calls=%async_computation.10 | async-start | bytes 1327104 | tf_op jit(solution)/shard_map/all_gather | solution.py:71
  10.1 213.0 %all-gather.23.cloned.1.call-start = ((), (), s32[]{:S(2)}) async-start(), calls=%async_computation.11 | async-start | bytes 5308416 | tf_op jit(solution)/shard_map/all_gather | solution.py:77
  14.0 6.7 %copy-start.3 = (f32[128,768]{1,0:T(8,128)S(1)}, f32[128,768]{1,0:T(8,128)}, u32[]{:S(2)}) copy-start(f32[128,768]{1,0:T(8,128)} %param.18) | copy-start | bytes 1179652
  14.0 7.4 %copy-start.41 = (u32[32]{0:T(128)S(1)}, u32[32]{0:T(128)}, u32[]{:S(2)}) copy-start(u32[32]{0:T(128)} %constant.89) | copy-start | bytes 388
  14.0 8.7 %copy-start.46 = (f32[1,96]{1,0:T(1,128)S(1)}, f32[1,96]{1,0:T(1,128)}, u32[]{:S(2)}) copy-start(f32[1,96]{1,0:T(1,128)} %param.23) | copy-start | bytes 1156
  14.0 9.0 %copy-start.47 = (f32[1,96]{1,0:T(1,128)S(1)}, f32[1,96]{1,0:T(1,128)}, u32[]{:S(2)}) copy-start(f32[1,96]{1,0:T(1,128)} %param.22) | copy-start | bytes 1156
  14.0 9.2 %copy-start.48 = (f32[1,96]{1,0:T(1,128)S(1)}, f32[1,96]{1,0:T(1,128)}, u32[]{:S(2)}) copy-start(f32[1,96]{1,0:T(1,128)} %param.20) | copy-start | bytes 1156
  14.0 9.4 %copy-start.49 = (f32[1,96]{1,0:T(1,128)S(1)}, f32[1,96]{1,0:T(1,128)}, u32[]{:S(2)}) copy-start(f32[1,96]{1,0:T(1,128)} %param.19) | copy-start | bytes 1156
  14.0 9.7 %copy-start.50 = (f32[1,96]{1,0:T(1,128)S(1)}, f32[1,96]{1,0:T(1,128)}, u32[]{:S(2)}) copy-start(f32[1,96]{1,0:T(1,128)} %param.25) | copy-start | bytes 1156
  14.0 9.9 %copy-start.51 = (f32[1,96]{1,0:T(1,128)S(1)}, f32[1,96]{1,0:T(1,128)}, u32[]{:S(2)}) copy-start(f32[1,96]{1,0:T(1,128)} %param.27) | copy-start | bytes 1156
  14.0 10.1 %copy-start.52 = (f32[1,96]{1,0:T(1,128)S(1)}, f32[1,96]{1,0:T(1,128)}, u32[]{:S(2)}) copy-start(f32[1,96]{1,0:T(1,128)} %param.26) | copy-start | bytes 1156
  14.0 183.3 %copy-start.42 = (f32[1,384]{1,0:T(1,128)S(1)}, f32[1,384]{1,0:T(1,128)}, u32[]{:S(2)}) copy-start(f32[1,384]{1,0:T(1,128)} %param.29) | copy-start | bytes 4612
  14.0 197.0 %copy-start = (f32[128,768]{1,0:T(8,128)S(1)}, f32[128,768]{1,0:T(8,128)}, u32[]{:S(2)}) copy-start(f32[128,768]{1,0:T(8,128)} %param.16) | copy-start | bytes 1179652
  14.1 203.9 %all-to-all-start = ((bf16[8,96,3072]{2,1,0:T(8,128)(2,1)}), bf16[8,96,3072]{2,1,0:T(8,128)(2,1)}, u32[]{:S(2)}, u32[]{:S(2)}) async-start(bf16[8,96,3072]{2,1,0:T(8,128)(2,1)} %tile.2), calls=%async_computation | async-start | bytes 9437184 | tf_op jit(solution)/shard_map/all_to_all | solution.py:19
  20.6 191.4 %copy-start.40 = (s32[1,128]{1,0:T(1,128)S(1)}, s32[1,128]{1,0:T(1,128)}, u32[]{:S(2)}) copy-start(s32[1,128]{1,0:T(1,128)} %param.17) | copy-start | bytes 1540
  20.6 239.2 %all-gather.17.cloned.1.call-start = ((), (), s32[]{:S(2)}) async-start(), calls=%async_computation.8 | async-start | bytes 1769472 | tf_op jit(solution)/shard_map/all_gather | solution.py:266
  21.3 280.3 %reduce-scatter.6.cloned.1.call-start = ((), (), s32[]{:S(2)}) async-start(), calls=%async_computation.6 | async-start | bytes 1327104 | tf_op jit(solution)/shard_map/reduce_scatter | solution.py:99
  197.3 17.5 %copy-start.21 = (f32[768]{0:T(1024)}, f32[768]{0:T(1024)S(1)}, u32[]{:S(2)}) copy-start(f32[768]{0:T(1024)S(1)} %convert_element_type.293) | copy-start | bytes 9220
  211.1 6.9 %copy-start.23 = (f32[768]{0:T(1024)}, f32[768]{0:T(1024)S(1)}, u32[]{:S(2)}) copy-start(f32[768]{0:T(1024)S(1)} %convert_element_type.296) | copy-start | bytes 9220
  211.2 3.6 copy-start.25
  211.9 2.9 copy-start.30
  215.1 0.8 copy-start.4
  215.9 7.2 %copy-start.10 = (bf16[12,64,128]{2,1,0:T(8,128)(2,1)}, bf16[12,64,128]{2,1,0:T(8,128)(2,1)S(1)}, u32[]{:S(2)}) copy-start(bf16[12,64,128]{2,1,0:T(8,128)(2,1)S(1)} %convolution_convert_fusion.5) | copy-start | bytes 589828
  217.8 16.2 %copy-start.28 = (f32[128]{0:T(128)}, f32[128]{0:T(128)S(1)}, u32[]{:S(2)}) copy-start(f32[128]{0:T(128)S(1)} %broadcast_multiply_fusion) | copy-start | bytes 1540
  218.0 16.0 %copy-start.33 = (f32[128]{0:T(128)}, f32[128]{0:T(128)S(1)}, u32[]{:S(2)}) copy-start(f32[128]{0:T(128)S(1)} %fusion.40) | copy-start | bytes 1540
  218.0 5.2 %copy-start.16 = (bf16[128,768]{1,0:T(8,128)(2,1)S(1)}, bf16[128,768]{1,0:T(8,128)(2,1)}, u32[]{:S(2)}) copy-start(bf16[128,768]{1,0:T(8,128)(2,1)} %convert_element_type.269) | copy-start | bytes 589828
  229.0 4.9 %copy-start.6 = (bf16[128,3072]{1,0:T(8,128)(2,1)}, bf16[128,3072]{1,0:T(8,128)(2,1)S(1)}, u32[]{:S(2)}) copy-start(bf16[128,3072]{1,0:T(8,128)(2,1)S(1)} %get-tuple-element.122) | copy-start | bytes 2359300
  233.9 2.2 copy-start.11
  234.2 0.6 copy-start.38
  235.5 0.7 copy-start.12
  235.5 2.4 copy-start.2
  237.7 79.3 %reduce-scatter.4.cloned.1.call-start = ((), (), s32[]{:S(2)}) async-start(), calls=%async_computation.5 | async-start | bytes 3981312 | tf_op jit(solution)/shard_map/reduce_scatter | solution.py:90
  241.2 1.5 copy-start.5
  242.7 1.0 copy-start.22
  242.7 1.0 copy-start.26
  242.7 1.0 copy-start.31
  243.3 18.8 %copy-start.13 = (bf16[12,64,128]{2,1,0:T(8,128)(2,1)}, bf16[12,64,128]{2,1,0:T(8,128)(2,1)S(1)}, u32[]{:S(2)}) copy-start(bf16[12,64,128]{2,1,0:T(8,128)(2,1)S(1)} %fusion.31) | copy-start | bytes 589828
  246.8 1.1 copy-start.7
  246.8 1.1 copy-start.24
  246.8 1.1 copy-start.29
  246.8 1.1 copy-start.34
  246.9 125.9 %reduce-scatter.8.cloned.1.call-start = ((), (), s32[]{:S(2)}) async-start(), calls=%async_computation.7 | async-start | bytes 5308416 | tf_op jit(solution)/shard_map/reduce_scatter | solution.py:111
  251.7 1.1 copy-start.8
  252.8 6.7 %copy-start.53 = (f32[1,96]{1,0:T(1,128)S(1)}, f32[1,96]{1,0:T(1,128)}, u32[]{:S(2)}) copy-start(f32[1,96]{1,0:T(1,128)} %param.31) | copy-start | bytes 1156
  253.8 9.1 %copy-start.27 = (f32[128]{0:T(128)S(1)}, f32[128]{0:T(128)}, u32[]{:S(2)}) copy-start(f32[128]{0:T(128)} %copy-done.25) | copy-start | bytes 1540
  253.8 45.0 %all-to-all-start.1 = ((bf16[128,8,384]{2,0,1:T(8,128)(2,1)}), bf16[128,8,384]{2,0,1:T(8,128)(2,1)}, u32[]{:S(2)}, u32[]{:S(2)}) async-start(bf16[128,8,384]{2,0,1:T(8,128)(2,1)} %bitcast.127), calls=%async_computation.4 | async-start | bytes 1572864 | tf_op jit(solution)/shard_map/all_to_all | solution.py:265
  258.2 181.2 %all-reduce.22.cloned.1.call-start = ((), (), s32[]{:S(2)}) async-start(), calls=%async_computation.12 | async-start | bytes 3538944 | tf_op jit(solution)/shard_map/psum | solution.py:121
  259.8 1.7 copy-start.37
  262.9 4.8 %copy-start.35 = (bf16[768]{0:T(1024)(128)(2,1)S(1)}, bf16[768]{0:T(1024)(128)(2,1)}, u32[]{:S(2)}) copy-start(bf16[768]{0:T(1024)(128)(2,1)} %get-tuple-element.56) | copy-start | bytes 4612
  262.9 4.8 %copy-start.36 = (bf16[768]{0:T(1024)(128)(2,1)S(1)}, bf16[768]{0:T(1024)(128)(2,1)}, u32[]{:S(2)}) copy-start(bf16[768]{0:T(1024)(128)(2,1)} %get-tuple-element.70) | copy-start | bytes 4612
  263.0 35.9 %copy-start.1 = (bf16[1024,768]{1,0:T(8,128)(2,1)S(1)}, bf16[1024,768]{1,0:T(8,128)(2,1)}, u32[]{:S(2)}) copy-start(bf16[1024,768]{1,0:T(8,128)(2,1)} %all-gather.17.cloned.1.call-done) | copy-start | bytes 4718596
  301.6 71.5 %copy-start.45 = (bf16[1,96]{1,0:T(2,128)(2,1)S(1)}, bf16[1,96]{1,0:T(2,128)(2,1)}, u32[]{:S(2)}) copy-start(bf16[1,96]{1,0:T(2,128)(2,1)} %convert_bitcast_fusion.1) | copy-start | bytes 580
  301.6 86.2 %copy-start.44 = (f32[128]{0:T(128)S(1)}, f32[128]{0:T(128)}, u32[]{:S(2)}) copy-start(f32[128]{0:T(128)} %copy-done.43) | copy-start | bytes 1540
  301.6 86.2 %copy-start.54 = (f32[128]{0:T(128)S(1)}, f32[128]{0:T(128)}, u32[]{:S(2)}) copy-start(f32[128]{0:T(128)} %get-tuple-element.69) | copy-start | bytes 1540
  301.6 86.2 %copy-start.19 = (f32[128,768]{1,0:T(8,128)S(1)}, f32[128,768]{1,0:T(8,128)}, u32[]{:S(2)}) copy-start(f32[128,768]{1,0:T(8,128)} %get-tuple-element.120) | copy-start | bytes 1179652
  301.6 86.2 %copy-start.32 = (f32[128]{0:T(128)S(1)}, f32[128]{0:T(128)}, u32[]{:S(2)}) copy-start(f32[128]{0:T(128)} %copy-done.30) | copy-start | bytes 1540
  301.6 86.5 %copy-start.39 = (f32[128]{0:T(128)S(1)}, f32[128]{0:T(128)}, u32[]{:S(2)}) copy-start(f32[128]{0:T(128)} %copy-done.38) | copy-start | bytes 1540
  372.8 16.2 %copy-start.9 = (bf16[128,3072]{1,0:T(8,128)(2,1)S(1)}, bf16[128,3072]{1,0:T(8,128)(2,1)}, u32[]{:S(2)}) copy-start(bf16[128,3072]{1,0:T(8,128)(2,1)} %get-tuple-element.115) | copy-start | bytes 2359300
  439.4 3.7 copy-start.18
  439.4 4.8 %copy-start.17 = (bf16[1,384,768]{2,1,0:T(8,128)(2,1)S(1)}, bf16[1,384,768]{2,1,0:T(8,128)(2,1)}, u32[]{:S(2)}) copy-start(bf16[1,384,768]{2,1,0:T(8,128)(2,1)} %get-tuple-element.100) | copy-start | bytes 1769476
  (1 other events, 0.5 us)
Sparse Core Ops, SparseCore 0:
  10.2 72.3 all-gather.18
  84.8 60.3 all-gather.20
  147.4 56.1 all-gather.22
  205.7 24.0 all-gather.16
  237.8 32.7 reduce-scatter.5
  272.8 44.1 reduce-scatter.3
  319.3 53.3 reduce-scatter.7
  376.8 62.6 all-reduce.21
